TPU v7x, 256 devices: a whole 4x4x8 slice. The times are simulated.
256 devices in a mesh: req: 16 (over y, x), kv: 8 (over z), blk: 2 (over core).
Axes of the slice: x: 4, y: 4, z: 8, core: 2. Of those that a mesh axis runs over, the one named last changes fastest.
Arguments:
- x_resid: bfloat16 [16, 256, 5120], P('req', ('kv', 'blk')), may hold values from -54 to 54
- q_new: bfloat16 [16, 256, 4096], P('req', None, 'kv'), may hold values from -36 to 36
- k_new: bfloat16 [16, 256, 1024], P('req', None, 'kv'), may hold values from -6 to 12
- v_new: bfloat16 [16, 256, 1024], P('req', None, 'kv'), may hold values from -24 to 24
- k_cache: bfloat16 [16, 8, 64, 128, 128], P('req', 'kv', 'blk'), may hold values from -6 to 12
- v_cache: bfloat16 [16, 8, 64, 128, 128], P('req', 'kv', 'blk'), may hold values from -24 to 24
- cache_len: int32 [16], P('req'), may hold values from 1 to 7936, as said below
- page_table: int32 [16, 64], P('req'), may hold values from 0 to 63, as said below
- wo: bfloat16 [4096, 5120], P(('kv', 'blk')), may hold values from -0.09375 to 0.09375
- norm_gain: bfloat16 [5120], replicated, may hold values from 0.099609375 to 1.8984375
- w_gate: bfloat16 [5120, 7168], P('req', ('kv', 'blk')), may hold values from -0.078125 to 0.078125
- w_up: bfloat16 [5120, 7168], P('req', ('kv', 'blk')), may hold values from -0.078125 to 0.078125
- w_down: bfloat16 [7168, 5120], P(('kv', 'blk'), 'req'), may hold values from -0.0625 to 0.0625
Outputs:
- layer_out: bfloat16 [16, 256, 5120], P('req', ('kv', 'blk'))
- k_cache_out: bfloat16 [16, 8, 64, 128, 128], P('req', 'kv', 'blk')
- v_cache_out: bfloat16 [16, 8, 64, 128, 128], P('req', 'kv', 'blk')
Inputs may be any that keep to these rules, and one draw needn't show every extreme that they name: `cache_len`: at least one request has the largest length. `page_table`: each row is a permutation of 0 to 63.
All inputs are finite; a program needn't handle non-finite values.
Results may differ from a plain program's by a relative error of at most 0.0095.
Values may be sent and summed in bfloat16 or wider, within the bound.
A program may use at most 128 MiB of HBM per device.

v0:
```python
import math

import jax
import jax.numpy as jnp
from jax import lax
from jax.sharding import PartitionSpec as P


def combined_all(part, axis, combine):
    gathered = jax.tree.map(lambda a: lax.all_gather(a, axis), part)

    def take(source):
        return jax.tree.map(lambda a: lax.dynamic_index_in_dim(a, source, 0, False), gathered)

    return lax.fori_loop(
        1, lax.axis_size(axis), lambda source, state: combine(state, take(source)), take(0)
    )


def rotate(field, positions):
    half_width = field.shape[-1] // 2
    pair_index = jnp.arange(half_width, dtype=jnp.float32)
    frequency = jnp.power(1000000.0, -2.0 * pair_index / field.shape[-1])
    angles = positions.astype(jnp.float32)[:, None] * frequency[None, :]
    cosine = jnp.cos(angles)
    sine_part = jnp.sin(angles)
    lower_half = field[..., :half_width]
    upper_half = field[..., half_width:]
    return jnp.concatenate(
        [
            lower_half * cosine - upper_half * sine_part,
            upper_half * cosine + lower_half * sine_part,
        ],
        axis=-1,
    )


def merge_parts(first_part, second_part):
    max_first, total_first, out_first = first_part
    max_second, total_second, out_second = second_part
    overall = jnp.maximum(max_first, max_second)
    factor_first = jnp.exp(max_first - overall)
    factor_second = jnp.exp(max_second - overall)
    return (
        overall,
        factor_first * total_first + factor_second * total_second,
        factor_first[..., None] * out_first + factor_second[..., None] * out_second,
    )


def fetch_down(w_down):
    return lax.all_gather(w_down, "req", axis=1, tiled=True)


def rms_rows(rows, norm_gain):
    return (
        rows
        * lax.rsqrt(jnp.mean(rows * rows, axis=-1, keepdims=True) + 1e-05)
        * norm_gain.astype(jnp.float32)
    ).astype(jnp.bfloat16)


def on_device(
    x_resid,
    q_new,
    k_new,
    v_new,
    k_cache,
    v_cache,
    cache_len,
    page_table,
    wo,
    norm_gain,
    w_gate,
    w_up,
    w_down,
):
    blk_count = lax.axis_size("blk")
    blk_id = lax.axis_index("blk")
    new_tokens = q_new.shape[1]
    head_dim = k_new.shape[2]
    group_size = q_new.shape[2] // head_dim
    slot_count = k_cache.shape[2]
    page_size = k_cache.shape[3]
    page_total = page_table.shape[1]
    length = cache_len[0]
    positions = length + jnp.arange(new_tokens, dtype=jnp.int32)
    query_heads = rotate(
        q_new[0].reshape(new_tokens, group_size, head_dim).astype(jnp.float32).transpose(1, 0, 2),
        positions,
    ).astype(jnp.bfloat16)
    fresh_keys = rotate(k_new[0].astype(jnp.float32), positions).astype(jnp.bfloat16)
    page_ids = jnp.arange(page_total, dtype=jnp.int32)
    physical = blk_id * slot_count + jnp.arange(slot_count, dtype=jnp.int32)
    logical = jnp.sum(
        jnp.where(page_table[0][None, :] == physical[:, None], page_ids[None, :], 0), axis=1
    )
    slot_position = (
        logical[:, None] * page_size + jnp.arange(page_size, dtype=jnp.int32)[None, :]
    ).reshape(slot_count * page_size)
    new_index = slot_position - length
    is_new = (new_index >= 0) & (new_index < new_tokens)
    chosen = jnp.clip(new_index, 0, new_tokens - 1)
    key_rows = jnp.where(
        is_new[:, None], fresh_keys[chosen], k_cache[0, 0].reshape(slot_count * page_size, head_dim)
    )
    value_rows = jnp.where(
        is_new[:, None], v_new[0][chosen], v_cache[0, 0].reshape(slot_count * page_size, head_dim)
    )
    scores = jnp.einsum(
        "qd,sd->qs",
        query_heads.reshape(group_size * new_tokens, head_dim),
        key_rows,
        preferred_element_type=jnp.float32,
    ) * (1.0 / math.sqrt(head_dim))
    scores = scores.reshape(group_size, new_tokens, slot_count * page_size)
    allowed = slot_position[None, None, :] <= positions[None, :, None]
    masked = jnp.where(allowed, scores, -1e30)
    block_max = jnp.max(masked, axis=-1)
    weights = jnp.where(allowed, jnp.exp(masked - block_max[..., None]), 0.0).astype(jnp.bfloat16)
    block_total = jnp.sum(weights.astype(jnp.float32), axis=-1)
    block_out = jnp.einsum("gcs,sd->gcd", weights, value_rows, preferred_element_type=jnp.float32)
    merged = combined_all((block_max, block_total, block_out), "blk", merge_parts)
    attn = (merged[2] / merged[1][..., None]).astype(jnp.bfloat16)
    per_core = group_size // blk_count
    mine = lax.dynamic_slice_in_dim(attn, blk_id * per_core, per_core, 0)
    mine_rows = mine.transpose(1, 0, 2).reshape(new_tokens, per_core * head_dim)
    token_rows = x_resid.shape[1]
    row_start = lax.axis_index(("kv", "blk")) * token_rows
    partial_value = jnp.dot(mine_rows, wo, preferred_element_type=jnp.float32)
    own_part = lax.dynamic_slice_in_dim(partial_value, row_start, token_rows, 0) + x_resid[
        0
    ].astype(jnp.float32)
    contrib = lax.dynamic_update_slice_in_dim(partial_value, own_part, row_start, 0)
    resid = lax.psum(contrib, ("kv", "blk"))
    normed = rms_rows(resid, norm_gain)
    own_resid = lax.dynamic_slice_in_dim(resid, row_start, token_rows, 0)
    gate_val = jnp.dot(
        normed,
        lax.all_gather(w_gate, "req", axis=0, tiled=True),
        preferred_element_type=jnp.float32,
    )
    up_val = jnp.dot(
        normed, lax.all_gather(w_up, "req", axis=0, tiled=True), preferred_element_type=jnp.float32
    )
    hidden = (jax.nn.silu(gate_val) * up_val).astype(jnp.bfloat16)
    down_full = fetch_down(w_down)
    mlp_rows = lax.psum_scatter(
        jnp.dot(hidden, down_full, preferred_element_type=jnp.float32).astype(jnp.bfloat16),
        ("kv", "blk"),
        scatter_dimension=0,
        tiled=True,
    ).astype(jnp.float32)
    layer_out = (own_resid + mlp_rows).astype(jnp.bfloat16)[None]
    return (layer_out, key_rows.reshape(k_cache.shape), value_rows.reshape(v_cache.shape))


def solution(mesh):
    in_specs = (
        P("req", ("kv", "blk"), None),
        P("req", None, "kv"),
        P("req", None, "kv"),
        P("req", None, "kv"),
        P("req", "kv", "blk", None, None),
        P("req", "kv", "blk", None, None),
        P("req"),
        P("req", None),
        P(("kv", "blk"), None),
        P(),
        P("req", ("kv", "blk")),
        P("req", ("kv", "blk")),
        P(("kv", "blk"), "req"),
    )
    out_specs = (
        P("req", ("kv", "blk"), None),
        P("req", "kv", "blk", None, None),
        P("req", "kv", "blk", None, None),
    )
    return jax.shard_map(
        on_device, mesh=mesh, in_specs=in_specs, out_specs=out_specs, check_vma=False
    )
```

profile of v0, /device:TPU:32, one launch (start us, length us, event | category | flops | bytes accessed | tf_op | source)
XLA Modules:
  0.0 361.4 jit_solution(288112992523952814)
XLA Ops:
  8.9 0.9 copy.31
  9.9 0.3 multiply_cosine_fusion
  10.3 0.8 select_reduce_fusion
  11.4 1.9 reshape.295
  13.3 1.3 copy.30
  14.8 15.0 %gather_fusion = bf16[4096,128]{1,0:T(8,128)(2,1)} fusion(bf16[256,128]{1,0:T(8,128)(2,1)S(1)} %copy.32, s32[4096]{0:T(1024)S(1)} %broadcast_clamp_fusion), kind=kCustom, calls=%fused_computation | custom fusion | bytes 2113536 | tf_op jit(solution)/shard_map/gather | solution.py:105
  29.8 15.0 %gather_fusion.1 = bf16[4096,128]{1,0:T(8,128)(2,1)} fusion(bf16[256,128]{1,0:T(8,128)(2,1)S(1)} %bitcast.87, s32[4096]{0:T(1024)S(1)} %broadcast_clamp_fusion), kind=kCustom, calls=%fused_computation.1 | custom fusion | bytes 2113536 | tf_op jit(solution)/shard_map/gather | solution.py:108
  44.9 0.6 broadcast_compare_fusion
  45.6 3.6 bitcast_select_fusion.2
  49.2 3.7 %fusion.1 = (f32[1024]{0:T(1024)S(1)}, f32[1024,4096]{1,0:T(8,128)S(1)}) fusion(pred[256,4096]{1,0:T(8,128)(4,1)S(1)} %broadcast_compare_fusion, bf16[4096,128]{1,0:T(8,128)(2,1)S(1)} %bitcast_select_fusion.2, bf16[1024,64]{0,1:T(8,128)(2,1)S(1)} %bitcast.95, bf16[1024,64]{0,1:T(8,128)(2,1)S(1)} %bitcast.94), kind=kOutput, calls=%fused_computation.6 | convolution fusion | flops 1086848000 | bytes 19140608 | tf_op jit(solution)/shard_map/qd,sd->qs/dot_general | solution.py:110
  52.9 6.7 %convert_reduce_fusion = (f32[1024]{0:T(1024)S(1)}, bf16[1024,4096]{1,0:T(8,128)(2,1)S(1)}) fusion(f32[1024]{0:T(1024)S(1)} %get-tuple-element.46, f32[1024,4096]{1,0:T(8,128)S(1)} %get-tuple-element.47, pred[256,4096]{1,0:T(8,128)(4,1)S(1)} %broadcast_compare_fusion), kind=kLoop, calls=%fused_computation.5 | loop fusion | flops 29359104 | bytes 26222592 | tf_op jit(solution)/shard_map/reduce_sum | solution.py:121
  59.7 1.5 broadcast_select_fusion
  61.2 1.0 copy-done.6
  62.2 3.2 fusion.34
  65.4 1.8 all_gather.32
  67.3 2.0 all_gather.28
  69.3 13.2 %all-gather.12.cloned.1.call-done = f32[8,256,128]{2,1,0:T(8,128)} async-done(((f32[4,256,128]{2,1,0:T(8,128)}), f32[8,256,128]{2,1,0:T(8,128)}) %all-gather.12.cloned.1.call-update) | async-done | bytes 1048592 | tf_op jit(solution)/shard_map/all_gather | solution.py:10
  82.5 1.3 fusion.33
  83.8 0.8 copy.37
  84.8 1.0 divide_convert_fusion
  85.8 3.2 fusion.35
  89.0 1.7 fusion.8
  90.8 0.5 all-gather.6.cloned.1.call-update
  91.4 0.5 all-gather.10.cloned.1.call-update
  92.0 0.5 all-gather.8.cloned.1.call-update
  92.6 123.6 %all-reduce.2.cloned.1.call-done = f32[256,5120]{1,0:T(8,128)} async-done(((f32[256,5120]{1,0:T(8,128)}), f32[256,5120]{1,0:T(8,128)}) %all-reduce.2.cloned.1.call-update) | async-done | bytes 5242896 | tf_op jit(solution)/shard_map/psum | solution.py:135
  216.2 2.9 multiply_reduce_fusion
  219.1 6.2 %fusion.29 = f32[256,448]{0,1:T(8,128)S(1)} fusion(bf16[5120,448]{1,0:T(8,128)(2,1)} %all-gather.6.cloned.1.call-done, f32[256,5120]{1,0:T(8,128)} %all-reduce.2.cloned.1.call-done, f32[5120]{0:T(1024)S(1)} %convert_element_type.69, f32[256]{0:T(256)S(1)} %add_rsqrt_fusion), kind=kOutput, calls=%fused_computation.74 | convolution fusion | flops 1178337280 | bytes 10310656 | tf_op jit(solution)/shard_map/dot_general | solution.py:138
  225.3 57.1 %all-gather.8.cloned.1.call-done = bf16[5120,448]{1,0:T(8,128)(2,1)} async-done(((bf16[320,448]{1,0:T(8,128)(2,1)}), bf16[5120,448]{1,0:T(8,128)(2,1)}) %all-gather.8.cloned.1.call-update) | async-done | bytes 4587536 | tf_op jit(solution)/shard_map/all_gather | solution.py:144
  282.4 12.4 %convolution_convert_fusion = bf16[256,5120]{1,0:T(8,128)(2,1)} fusion(bf16[448,5120]{0,1:T(8,128)(2,1)} %all-gather.10.cloned.1.call-done, bf16[5120,448]{1,0:T(8,128)(2,1)} %all-gather.8.cloned.1.call-done, f32[256,448]{0,1:T(8,128)S(1)} %fusion.29, f32[256,5120]{1,0:T(8,128)} %all-reduce.2.cloned.1.call-done, f32[5120]{0:T(1024)S(1)} %convert_element_type.69, ...), kind=kOutput, calls=%fused_computation.7 | convolution fusion | flops 2354741248 | bytes 17519616 | tf_op jit(solution)/shard_map/dot_general | solution.py:149
  294.8 57.5 %reduce-scatter.2.cloned.1.call-done = bf16[16,5120]{1,0:T(8,128)(2,1)} async-done(((bf16[256,5120]{1,0:T(8,128)(2,1)}), bf16[16,5120]{1,0:T(8,128)(2,1)}) %reduce-scatter.2.cloned.1.call-update) | async-done | bytes 163856 | tf_op jit(solution)/shard_map/reduce_scatter | solution.py:148
  352.3 1.8 fusion.14
  (54 shorter events, 1.2 us)
Async XLA Ops:
  8.0 77.8 %copy-start = (bf16[256,5120]{1,0:T(8,128)(2,1)S(1)}, bf16[256,5120]{1,0:T(8,128)(2,1)}, u32[]{:S(2)}) copy-start(bf16[256,5120]{1,0:T(8,128)(2,1)} %param.21) | copy-start | bytes 7864324
  8.0 74.5 %all-gather.12.cloned.1.call-start = ((), (), s32[]{:S(2)}) async-start(), calls=%async_computation.6 | async-start | bytes 1572864 | tf_op jit(solution)/shard_map/all_gather | solution.py:10
  14.6 15.2 %copy-start.1 = (bf16[1,256,128]{2,1,0:T(8,128)(2,1)S(1)}, bf16[1,256,128]{2,1,0:T(8,128)(2,1)}, u32[]{:S(2)}) copy-start(bf16[1,256,128]{2,1,0:T(8,128)(2,1)} %param.16) | copy-start | bytes 196612
  52.9 6.8 %copy-start.2 = (bf16[4096,128]{1,0:T(8,128)(2,1)S(1)}, bf16[4096,128]{1,0:T(8,128)(2,1)}, u32[]{:S(2)}) copy-start(bf16[4096,128]{1,0:T(8,128)(2,1)} %gather_fusion) | copy-start | bytes 3145732
  52.9 6.8 %copy-start.3 = (bf16[4096,128]{1,0:T(8,128)(2,1)S(1)}, bf16[4096,128]{1,0:T(8,128)(2,1)}, u32[]{:S(2)}) copy-start(bf16[4096,128]{1,0:T(8,128)(2,1)} %gather_fusion.1) | copy-start | bytes 3145732
  52.9 6.8 %copy-start.4 = (bf16[1,1,32,128,128]{4,3,2,1,0:T(8,128)(2,1)S(1)}, bf16[1,1,32,128,128]{4,3,2,1,0:T(8,128)(2,1)}, u32[]{:S(2)}) copy-start(bf16[1,1,32,128,128]{4,3,2,1,0:T(8,128)(2,1)} %param.17) | copy-start | bytes 3145732
  52.9 6.8 %copy-start.5 = (bf16[1,1,32,128,128]{4,3,2,1,0:T(8,128)(2,1)S(1)}, bf16[1,1,32,128,128]{4,3,2,1,0:T(8,128)(2,1)}, u32[]{:S(2)}) copy-start(bf16[1,1,32,128,128]{4,3,2,1,0:T(8,128)(2,1)} %param.18) | copy-start | bytes 3145732
  61.2 1.0 copy-start.6
  65.4 150.8 %all-reduce.2.cloned.1.call-start = ((), (), s32[]{:S(2)}) async-start(), calls=%async_computation.1 | async-start | bytes 10485760 | tf_op jit(solution)/shard_map/psum | solution.py:135
  84.7 4.4 %copy-start.7 = (bf16[1,16,5120]{2,1,0:T(8,128)(2,1)S(1)}, bf16[1,16,5120]{2,1,0:T(8,128)(2,1)}, u32[]{:S(2)}) copy-start(bf16[1,16,5120]{2,1,0:T(8,128)(2,1)} %param.13) | copy-start | bytes 491524
  89.0 3.6 copy-start.8
  90.8 128.4 %all-gather.6.cloned.1.call-start = ((), (), s32[]{:S(2)}) async-start(), calls=%async_computation.2 | async-start | bytes 5570560 | tf_op jit(solution)/shard_map/all_gather | solution.py:140
  91.4 134.0 %all-gather.10.cloned.1.call-start = ((), (), s32[]{:S(2)}) async-start(), calls=%async_computation.4 | async-start | bytes 5570560 | tf_op jit(solution)/shard_map/all_gather | solution.py:52
  92.0 190.5 %all-gather.8.cloned.1.call-start = ((), (), s32[]{:S(2)}) async-start(), calls=%async_computation.3 | async-start | bytes 5570560 | tf_op jit(solution)/shard_map/all_gather | solution.py:144
  92.5 259.8 %reduce-scatter.2.cloned.1.call-start = ((), (), s32[]{:S(2)}) async-start(), calls=%async_computation.5 | async-start | bytes 2785280 | tf_op jit(solution)/shard_map/reduce_scatter | solution.py:148
Sparse Core Ops, SparseCore 0:
  65.5 16.9 all-gather.11
  90.9 125.2 all-reduce.1
  294.9 57.3 reduce-scatter.1
Sparse Core Ops, SparseCore 1:
  93.7 62.4 all-gather.5
  158.4 60.7 all-gather.9
  221.5 60.8 all-gather.7
where the time goes:
time: 365 us; the launch traced here: 361 us
  waiting for transfers between devices  253 us (69%)
  local copies, waits for them, and re-layouts  37.7 us (10%)
  matrix products  28.6 us (8%)
  other arithmetic  21.5 us (6%)
  between operations  16.6 us (5%)
  blocking collectives  3.81 us (1%)
    psum x1, waiting for transfers between devices, on_device(): resid = lax.psum(contrib, ('kv', 'blk'))  124 us
    reduce_scatter x1, waiting for transfers between devices, on_device(): lax.psum_scatter(jnp.dot(hidden, down_full, preferred_element_type=jnp.fl...  57.5 us
    all_gather x1, waiting for transfers between devices, on_device(): lax.all_gather(w_up, 'req', axis=0, tiled=True)  57.1 us
    gather x1, local copies, waits for them, and re-layouts, on_device(): fresh_keys[chosen]  15 us
    gather x1, local copies, waits for them, and re-layouts, on_device(): v_new[0][chosen]  15 us
    all_gather x1, waiting for transfers between devices, combined_all(): gathered = jax.tree.map(lambda a: lax.all_gather(a, axis), part)  13.2 us
    dot_general x1, matrix products, on_device(): jnp.dot(hidden, down_full, preferred_element_type=jnp.float32)  12.4 us
  transfers between devices with their start and end apart: 6, of which 4 were waited for; matrix products, arithmetic and copies ran while one was open for 3% of the time, Pallas kernels for 0%

commit v1 on v0

v1 whole, which is shorter than its diff:
```python
import functools
import math

import jax
import jax.numpy as jnp
from jax import lax
from jax.experimental import pallas as pl
from jax.experimental.pallas import tpu as pltpu
from jax.sharding import PartitionSpec as P

MESH = pl.DeviceIdType.MESH
SIDE = 4
RING = 8
ROWS = 16
BF16, F32 = jnp.bfloat16, jnp.float32


def torus_plan():
    entries, got = [], {}

    def add(rnd, offset, first, count, direction):
        need = sorted({got[offset, q] for q in range(first, first + count)}) if offset != (0, 0) else []
        there = tuple((o - d) % SIDE for o, d in zip(offset, direction))
        for q in range(first, first + count):
            assert (there, q) not in got and there != (0, 0)
            got[there, q] = len(entries)
        entries.append((rnd, offset, first, count, direction, need))

    east, west, north, south = (1, 0), (-1, 0), (0, 1), (0, -1)
    for direction in (east, west, north, south):
        add(0, (0, 0), 0, 4, direction)
    for offset, half, quarters, ahead, across in (
        ((1, 0), 0, (0, 2), west, (north, south)),
        ((3, 0), 0, (1, 3), east, (north, south)),
        ((0, 1), 2, (0, 2), south, (east, west)),
        ((0, 3), 2, (1, 3), north, (east, west)),
    ):
        for direction in across:
            add(1, offset, half, 2, direction)
        for quarter in quarters:
            add(1, offset, quarter, 1, ahead)
    for direction in (north, south):
        add(2, (2, 0), 0, 2, direction)
    for direction in (east, west):
        add(2, (0, 2), 2, 2, direction)
    for offset in ((1, 1), (3, 1), (1, 3), (3, 3)):
        add(2, offset, *((0, 1, south) if offset[1] == 1 else (1, 1, north)))
        add(2, offset, *((2, 1, west) if offset[0] == 1 else (3, 1, east)))
    add(3, (2, 1), 0, 1, south)
    add(3, (2, 3), 1, 1, north)
    add(3, (1, 2), 2, 1, west)
    add(3, (3, 2), 3, 1, east)
    assert len(got) == 4 * (SIDE * SIDE - 1)
    return entries


PLAN = torus_plan()
STREAMS = ((1, 0, 4), (-1, 1, 4), (-1, 0, 3), (1, 1, 3))
BASE = (0, 4, 8, 11)
SLOTS_Z = 14


def kernel(
    q_ref, rel_ref, x_ref, gain_ref, k_hbm, v_hbm, wo_hbm, gu_hbm, dt_hbm,
    out_ref,
    k_vm, v_vm, wo_vm, gu_vm, dt_vm, mine, theirs, sent, attn, pb, nb, acc, hid, resid,
    snd, rcv, snd2, rcv2, xs, xr,
    local_sem, gu_s, gu_r, dt_s, dt_r, one_s, one_r, z1_s, z1_r, zg_s, zg_r, z2_s, z2_r, chip_s, chip_r, ex_s, ex_r,
):
    req, kz, core = lax.axis_index("req"), lax.axis_index("kv"), lax.axis_index("blk")
    other = 1 - core
    mx, my = lax.rem(req, SIDE), lax.div(req, SIDE)
    width = pb.shape[2]
    half = width // 2
    quarter = width // 4
    heads = q_ref.shape[1]
    half_tokens = q_ref.shape[2]
    head_dim = q_ref.shape[3]
    partner = (req, kz, other)

    def plane(offset):
        x = lax.rem(mx + (offset[0] % SIDE), SIDE)
        y = lax.rem(my + (offset[1] % SIDE), SIDE)
        return y * SIDE + x

    def ring(step):
        return lax.rem(kz + (step % RING), RING)

    pending = []

    def send(src, dst, ssem, rsem, device):
        copy = pltpu.make_async_remote_copy(
            src_ref=src, dst_ref=dst, send_sem=ssem, recv_sem=rsem, device_id=device, device_id_type=MESH
        )
        copy.start()
        pending.append(copy)

    def arrive(dst, ssem, rsem, device):
        pltpu.make_async_remote_copy(
            src_ref=dst, dst_ref=dst, send_sem=ssem, recv_sem=rsem, device_id=device, device_id_type=MESH
        ).wait_recv()

    shard = gu_hbm.shape[0]
    part = shard // 4
    own_rows = pl.ds(pl.multiple_of(req * shard, 16), shard)
    wo_rows = wo_hbm.shape[0]
    local = [
        pltpu.make_async_copy(k_hbm, k_vm, local_sem.at[0]),
        pltpu.make_async_copy(v_hbm, v_vm, local_sem.at[1]),
        pltpu.make_async_copy(gu_hbm, gu_vm.at[own_rows], local_sem.at[2]),
        pltpu.make_async_copy(dt_hbm, dt_vm.at[own_rows], local_sem.at[3]),
        pltpu.make_async_copy(
            wo_hbm, wo_vm.at[pl.ds(pl.multiple_of(core * wo_rows, 16), wo_rows)], local_sem.at[4]
        ),
    ]
    for copy in local:
        copy.start()
    barrier = pltpu.get_barrier_semaphore()
    friends = [(plane(d), kz, core) for d in ((1, 0), (-1, 0), (0, 1), (0, -1))]
    friends += [(req, ring(1), core), (req, ring(-1), core), partner]
    for friend in friends:
        pl.semaphore_signal(barrier, inc=1, device_id=friend, device_id_type=MESH)
    pl.semaphore_wait(barrier, len(friends))

    stream = {"gu": (gu_hbm, gu_vm, gu_s, gu_r), "dt": (dt_hbm, dt_vm, dt_s, dt_r)}
    landed = {"gu": set(), "dt": set()}

    def rows_of(offset, first, count):
        start = plane(offset) * shard + first * part
        return pl.ds(pl.multiple_of(start, 16), count * part)

    def land(name, index):
        if index in landed[name]:
            return
        landed[name].add(index)
        _, full, ssem, rsem = stream[name]
        _, offset, first, count, direction, _ = PLAN[index]
        here = tuple((o - d) % SIDE for o, d in zip(offset, direction))
        back = tuple(-d for d in direction)
        arrive(full.at[rows_of(here, first, count)], ssem.at[index], rsem.at[index], (plane(back), kz, core))

    def issue(name, rnd):
        source, full, ssem, rsem = stream[name]
        for index, (when, offset, first, count, direction, need) in enumerate(PLAN):
            if when != rnd:
                continue
            for earlier in need:
                land(name, earlier)
            rows = rows_of(offset, first, count)
            src = source if offset == (0, 0) else full.at[rows]
            send(src, full.at[rows], ssem.at[index], rsem.at[index], (plane(direction), kz, core))

    issue("gu", 0)
    own_wo = wo_vm.at[pl.ds(pl.multiple_of(core * wo_rows, 16), wo_rows)]
    send(wo_hbm, own_wo, one_s.at[0], one_r.at[0], partner)
    issue("dt", 0)

    scale = 1.0 / math.sqrt(head_dim)
    local[0].wait()
    local[1].wait()

    def attend(part_id, result):
        row = lax.broadcasted_iota(jnp.int32, (half_tokens, 1), 0)
        token = (row // ROWS) * (2 * ROWS) + row % ROWS + part_id * ROWS
        lane = lax.broadcasted_iota(jnp.int32, (half_tokens, head_dim), 1)

        def head(g, carry):
            score = lax.dot_general(
                q_ref[part_id, g], k_vm[...], (((1,), (1,)), ((), ())), preferred_element_type=F32
            )
            allowed = rel_ref[...] <= token
            score = jnp.where(allowed, score * scale, -1e30)
            top = jnp.max(score, axis=-1, keepdims=True)
            weight = jnp.where(allowed, jnp.exp(score - top), 0.0)
            total = jnp.sum(weight, axis=-1, keepdims=True)
            result[g, :, :head_dim] = jnp.dot(weight.astype(BF16), v_vm[...], preferred_element_type=F32)
            result[g, :, head_dim:] = jnp.where(lane < head_dim // 2, top, total)
            return carry

        lax.fori_loop(0, heads, head, 0)

    attend(other, sent)
    send(sent, theirs, one_s.at[1], one_r.at[1], partner)
    attend(core, mine)
    arrive(theirs, one_s.at[1], one_r.at[1], partner)
    mid = head_dim + head_dim // 2
    for g in range(heads):
        a, b = mine[g], theirs[g]
        top_a, top_b = a[:, head_dim : head_dim + 1], b[:, head_dim : head_dim + 1]
        top = jnp.maximum(top_a, top_b)
        fa, fb = jnp.exp(top_a - top), jnp.exp(top_b - top)
        total = fa * a[:, mid : mid + 1] + fb * b[:, mid : mid + 1]
        value = (fa * a[:, :head_dim] + fb * b[:, :head_dim]) / total
        attn[:, g * head_dim : (g + 1) * head_dim] = value.astype(BF16)

    def columns(part_id):
        return slice(part_id * half, (part_id + 1) * half)

    def ring_send(s, j, out_buf, in_buf, ssem, rsem):
        direction, part_id, reach = STREAMS[s]
        slot = BASE[s] + j
        value = pb[ring(direction * (reach - j)), :, columns(part_id)]
        if j > 0:
            arrive(in_buf.at[slot - 1], ssem.at[slot - 1], rsem.at[slot - 1], (req, ring(-direction), core))
            value = value + in_buf[slot - 1].astype(F32)
        out_buf[slot] = value.astype(BF16)
        send(out_buf.at[slot], in_buf.at[slot], ssem.at[slot], rsem.at[slot], (req, ring(direction), core))

    def ring_total(part_id, in_buf, ssem, rsem):
        value = pb[kz, :, columns(part_id)]
        for s, (direction, p, reach) in enumerate(STREAMS):
            if p == part_id:
                slot = BASE[s] + reach - 1
                arrive(in_buf.at[slot], ssem.at[slot], rsem.at[slot], (req, ring(-direction), core))
                value = value + in_buf[slot].astype(F32)
        return value

    local[4].wait()
    theirs_wo = wo_vm.at[pl.ds(pl.multiple_of(other * wo_rows, 16), wo_rows)]
    arrive(theirs_wo, one_s.at[0], one_r.at[0], partner)
    for c in range(4):
        cols = slice(c * quarter, (c + 1) * quarter)
        block = jnp.dot(attn[...], wo_vm[:, cols], preferred_element_type=F32)
        pb[:, :, cols] = block.reshape(RING, ROWS, quarter)
        if c % 2 == 1:
            for s in range(4):
                if STREAMS[s][1] == c // 2:
                    ring_send(s, 0, snd, rcv, z1_s, z1_r)
    issue("gu", 1)
    for j in range(1, 4):
        for s in range(4):
            if j < STREAMS[s][2]:
                ring_send(s, j, snd, rcv, z1_s, z1_r)
    for p in range(2):
        resid[:, columns(p)] = ring_total(p, rcv, z1_s, z1_r) + x_ref[:, columns(p)].astype(F32)
    rows = resid[...]
    inverse = lax.rsqrt(jnp.mean(rows * rows, axis=-1, keepdims=True) + 1e-05)
    nb[kz] = (rows * inverse * gain_ref[...].astype(F32)).astype(BF16)

    def chip_send(step, part_id):
        slot = part_id * RING + step % RING
        block = ring(step)
        send(
            nb.at[block, :, columns(part_id)], nb.at[RING + block, :, columns(part_id)],
            chip_s.at[slot], chip_r.at[slot], partner,
        )

    def gather_arrive(s, j):
        direction, part_id, _ = STREAMS[s]
        slot = BASE[s] + j
        step = -direction * (j + 1)
        arrive(nb.at[ring(step), :, columns(part_id)], zg_s.at[slot], zg_r.at[slot], (req, ring(-direction), core))

    def gather_send(s, j):
        direction, part_id, _ = STREAMS[s]
        slot = BASE[s] + j
        block = nb.at[ring(-direction * j), :, columns(part_id)]
        send(block, block, zg_s.at[slot], zg_r.at[slot], (req, ring(direction), core))

    order = (0, 2, 1, 3)
    for s in order:
        gather_send(s, 0)
    for p in range(2):
        chip_send(0, p)
    for j in range(1, 4):
        for s in order:
            direction, part_id, reach = STREAMS[s]
            gather_arrive(s, j - 1)
            if j < reach:
                gather_send(s, j)
            chip_send(-direction * j, part_id)
        if j == 1:
            issue("gu", 2)
            issue("dt", 1)
    for s in (0, 1):
        direction, part_id, reach = STREAMS[s]
        gather_arrive(s, reach - 1)
        chip_send(-direction * reach, part_id)
    issue("gu", 3)
    local[2].wait()
    for index in range(len(PLAN)):
        land("gu", index)

    for c in range(4):
        if c % 2 == 0:
            for step in range(RING):
                slot = (c // 2) * RING + step
                block = nb.at[RING + ring(step), :, columns(c // 2)]
                arrive(block, chip_s.at[slot], chip_r.at[slot], partner)
        cols = slice(c * quarter, (c + 1) * quarter)
        value = jnp.dot(
            nb[:, :, cols].reshape(2 * RING * ROWS, quarter), gu_vm[cols, :], preferred_element_type=F32
        )
        if c == 0:
            acc[...] = value
        else:
            acc[...] += value
    units = hid.shape[1]
    whole = units // 128 * 128
    gate, up = acc[:, :whole], acc[:, whole + 128 :]
    hid[:, :whole] = (gate / (1.0 + jnp.exp(-gate)) * up).astype(BF16)
    gate = acc[:, whole : whole + 128]
    up = pltpu.roll(gate, 64, 1)
    tail = (gate / (1.0 + jnp.exp(-gate)) * up).astype(BF16)
    hid[:, whole:] = tail[:, : units - whole]

    issue("dt", 2)
    issue("dt", 3)
    local[3].wait()
    for index in range(len(PLAN)):
        land("dt", index)
    for c in range(4):
        cols = slice(c * quarter, (c + 1) * quarter)
        value = lax.dot_general(hid[...], dt_vm[cols, :], (((1,), (1,)), ((), ())), preferred_element_type=F32)
        pb[:, :, cols] = value[: RING * ROWS].reshape(RING, ROWS, quarter)
        xs[:, :, cols] = value[RING * ROWS :].astype(BF16).reshape(RING, ROWS, quarter)
        send(xs.at[:, :, cols], xr.at[:, :, cols], ex_s.at[c], ex_r.at[c], partner)
    for c in range(4):
        cols = slice(c * quarter, (c + 1) * quarter)
        arrive(xr.at[:, :, cols], ex_s.at[c], ex_r.at[c], partner)
        pb[:, :, cols] += xr[:, :, cols].astype(F32)
        if c % 2 == 1:
            for s in range(4):
                if STREAMS[s][1] == c // 2:
                    ring_send(s, 0, snd2, rcv2, z2_s, z2_r)
    for j in range(1, 4):
        for s in range(4):
            if j < STREAMS[s][2]:
                ring_send(s, j, snd2, rcv2, z2_s, z2_r)
    for p in range(2):
        out_ref[:, columns(p)] = (resid[:, columns(p)] + ring_total(p, rcv2, z2_s, z2_r)).astype(BF16)
    for copy in pending:
        copy.wait_send()


def layer(q, rel, x, gain, keys, values, wo, gate_up, down):
    width = x.shape[1]
    hidden = down.shape[1]
    slots = keys.shape[0]
    head_dim = keys.shape[1]
    heads, half_tokens = q.shape[1], q.shape[2]
    vmem = pl.BlockSpec(memory_space=pltpu.VMEM)
    hbm = pl.BlockSpec(memory_space=pl.ANY)
    dma = pltpu.SemaphoreType.DMA
    part = pltpu.VMEM((heads, half_tokens, 2 * head_dim), F32)
    hop = pltpu.VMEM((SLOTS_Z, ROWS, width // 2), BF16)
    plan = dma((len(PLAN),))
    return pl.pallas_call(
        kernel,
        out_shape=jax.ShapeDtypeStruct(x.shape, BF16),
        in_specs=[vmem] * 4 + [hbm] * 5,
        out_specs=vmem,
        scratch_shapes=[
            pltpu.VMEM((slots, head_dim), BF16),
            pltpu.VMEM((slots, head_dim), BF16),
            pltpu.VMEM((2 * wo.shape[0], width), BF16),
            pltpu.VMEM((width, gate_up.shape[1]), BF16),
            pltpu.VMEM((width, hidden), BF16),
            part, part, part,
            pltpu.VMEM((half_tokens, heads * head_dim), BF16),
            pltpu.VMEM((RING, ROWS, width), F32),
            pltpu.VMEM((2 * RING, ROWS, width), BF16),
            pltpu.VMEM((2 * RING * ROWS, gate_up.shape[1]), F32),
            pltpu.VMEM((2 * RING * ROWS, hidden), BF16),
            pltpu.VMEM((ROWS, width), F32),
            hop, hop, hop, hop,
            pltpu.VMEM((RING, ROWS, width), BF16),
            pltpu.VMEM((RING, ROWS, width), BF16),
            dma((5,)),
            plan, plan, plan, plan,
            dma((2,)), dma((2,)),
            dma((SLOTS_Z,)), dma((SLOTS_Z,)), dma((SLOTS_Z,)), dma((SLOTS_Z,)), dma((SLOTS_Z,)), dma((SLOTS_Z,)),
            dma((2 * RING,)), dma((2 * RING,)),
            dma((4,)), dma((4,)),
        ],
        compiler_params=pltpu.CompilerParams(
            collective_id=0, has_side_effects=True, vmem_limit_bytes=62 * 2**20
        ),
        name="layer",
    )(q, rel, x, gain, keys, values, wo, gate_up, down)


def rotate(field, positions):
    half_width = field.shape[-1] // 2
    pair_index = jnp.arange(half_width, dtype=F32)
    frequency = jnp.power(1000000.0, -2.0 * pair_index / field.shape[-1])
    angles = positions.astype(F32)[:, None] * frequency[None, :]
    cosine, sine = jnp.cos(angles)[:, None, :], jnp.sin(angles)[:, None, :]
    lower, upper = field[..., :half_width], field[..., half_width:]
    return jnp.concatenate([lower * cosine - upper * sine, upper * cosine + lower * sine], axis=-1)


def on_device(
    x_resid, q_new, k_new, v_new, k_cache, v_cache, cache_len, page_table, wo, norm_gain, w_gate, w_up, w_down
):
    blk_id = lax.axis_index("blk")
    new_tokens, head_dim = k_new.shape[1:]
    group = q_new.shape[2] // head_dim
    slot_count, page_size = k_cache.shape[2:4]
    page_total = page_table.shape[1]
    length = cache_len[0]
    positions = length + jnp.arange(new_tokens, dtype=jnp.int32)
    both = jnp.concatenate(
        [q_new[0].reshape(new_tokens, group, head_dim), k_new[0].reshape(new_tokens, 1, head_dim)], axis=1
    )
    turned = rotate(both.astype(F32), positions).astype(BF16)
    queries = turned[:, :group].reshape(RING, 2, ROWS, group, head_dim).transpose(1, 3, 0, 2, 4)
    queries = queries.reshape(2, group, new_tokens // 2, head_dim)

    first_page, shift = length // page_size, length % page_size
    images = 3
    fresh = jnp.concatenate([turned[:, group], v_new[0]], axis=1)
    place = jnp.arange(images * page_size, dtype=jnp.int32)[:, None]
    source = jnp.arange(new_tokens, dtype=jnp.int32)[None, :]
    moved = jnp.dot((place == source + shift).astype(BF16), fresh, preferred_element_type=F32).astype(BF16)
    moved = moved.reshape(images, page_size, 2 * head_dim)
    page_ids = jnp.arange(page_total, dtype=jnp.int32)
    physical = blk_id * slot_count + jnp.arange(slot_count, dtype=jnp.int32)
    logical = jnp.sum(jnp.where(page_table[0][None, :] == physical[:, None], page_ids[None, :], 0), axis=1)
    new_index = logical[:, None] * page_size + jnp.arange(page_size, dtype=jnp.int32)[None, :] - length
    is_new = ((new_index >= 0) & (new_index < new_tokens))[:, :, None]
    which = (logical - first_page)[:, None, None]

    def written(cache, columns):
        image = moved[:, :, columns]
        picked = jnp.where(which == 0, image[0], jnp.where(which == 1, image[1], image[2]))
        return jnp.where(is_new, picked, cache[0, 0])

    keys = written(k_cache, slice(0, head_dim))
    values = written(v_cache, slice(head_dim, 2 * head_dim))
    whole = w_gate.shape[1] // 128 * 128
    gate_up = jnp.concatenate([w_gate, w_up[:, whole:], w_up[:, :whole]], axis=1)
    layer_out = layer(
        queries,
        new_index.reshape(1, slot_count * page_size),
        x_resid[0],
        norm_gain[None],
        keys.reshape(slot_count * page_size, head_dim),
        values.reshape(slot_count * page_size, head_dim),
        wo,
        gate_up,
        w_down.T,
    )
    return (layer_out[None], keys[None, None], values[None, None])


def solution(mesh):
    in_specs = (
        P("req", ("kv", "blk"), None),
        P("req", None, "kv"),
        P("req", None, "kv"),
        P("req", None, "kv"),
        P("req", "kv", "blk", None, None),
        P("req", "kv", "blk", None, None),
        P("req"),
        P("req", None),
        P(("kv", "blk"), None),
        P(),
        P("req", ("kv", "blk")),
        P("req", ("kv", "blk")),
        P(("kv", "blk"), "req"),
    )
    out_specs = (
        P("req", ("kv", "blk"), None),
        P("req", "kv", "blk", None, None),
        P("req", "kv", "blk", None, None),
    )
    return jax.shard_map(on_device, mesh=mesh, in_specs=in_specs, out_specs=out_specs, check_vma=False)
```

time: 365 us -> 129 us (0.35); the launches traced: 361 us -> 129 us
  waiting for transfers between devices: 253 us -> 0 us
  Pallas kernels: 0 us -> 113 us
  local copies, waits for them, and re-layouts: 37.7 us -> 5.46 us
  matrix products: 28.6 us -> 0.25 us
  between operations: 16.6 us -> 1.57 us
  other arithmetic: 21.5 us -> 9.02 us
  blocking collectives: 3.81 us -> 0 us
    psum x1 -> x0, waiting for transfers between devices: 124 us -> none  [on_device(): resid = lax.psum(contrib, ('kv', 'blk'))]
    pallas_call x0 -> x1, Pallas kernels: none -> 113 us  [layer(): pl.pallas_call(kernel, out_shape=jax.ShapeDtypeStruct(x.shape, BF16), in_...]
    all_gather x4 -> x0, waiting for transfers between devices: 70.3 us -> none  [the longest x1 57.1 us: on_device(): lax.all_gather(w_up, 'req', axis=0, tiled=True)]
    reduce_scatter x1 -> x0, waiting for transfers between devices: 57.5 us -> none  [on_device(): lax.psum_scatter(jnp.dot(hidden, down_full, preferred_element_type=jnp.fl...]
    gather x2 -> x0, local copies, waits for them, and re-layouts: 30.1 us -> none  [the longest x1 15 us: on_device(): fresh_keys[chosen]]
    dot_general x5 -> x1, matrix products: 28.6 us -> 0.25 us  [on_device(): jnp.dot((place == source + shift).astype(BF16), fresh, preferred_element_...]
    reduce_sum x2 -> x0, other arithmetic: 9.63 us -> none  [the longest x1 6.71 us: on_device(): block_total = jnp.sum(weights.astype(jnp.float32), axis=-1)]
    all_gather x2 -> x0, blocking collectives: 3.81 us -> none  [combined_all(): gathered = jax.tree.map(lambda a: lax.all_gather(a, axis), part)]
  transfers between devices with their start and end apart: 6 -> 0, of which waited for: 4 -> 0; matrix products, arithmetic and copies ran while one was open for 3% -> 0% of each run, Pallas kernels for 0% -> 0%
where the time goes in v1:
time: 129 us
  Pallas kernels  113 us (88%)
  other arithmetic  9.02 us (7%)
  local copies, waits for them, and re-layouts  5.46 us (4%)
  between operations  1.57 us (1%)
    pallas_call x1, Pallas kernels, layer(): pl.pallas_call(kernel, out_shape=jax.ShapeDtypeStruct(x.shape, BF16), in_...  113 us
    select_n x2, other arithmetic, written(): return jnp.where(is_new, picked, cache[0, 0])  5.99 us
    unnamed x14, local copies, waits for them, and re-layouts  3.13 us

profile of v1, /device:TPU:32, one launch (start us, length us, event | category | flops | bytes accessed | tf_op | source)
XLA Modules:
  0.0 129.1 jit_solution(8723863101969354498)
XLA Ops:
  0.6 0.0 slice-start
  0.6 0.0 slice-start.1
  0.7 0.0 copy-start.3
  1.4 0.8 select_reduce_fusion
  2.3 0.1 broadcast_bitcast_fusion
  2.4 0.1 compare_and_fusion
  2.5 0.7 add_subtract_fusion
  3.1 1.3 %broadcast_in_dim.126.gain_ref = bf16[1,5120]{1,0:T(2,128)(2,1)} reshape(bf16[5120]{0:T(1024)(128)(2,1)} %param.22) | data formatting | bytes 20480 | tf_op jit(solution)/shard_map/broadcast_in_dim | solution.py:437
  4.5 0.0 copy-start.4
  4.5 1.0 copy.27
  5.5 0.9 copy.30
  6.4 0.3 multiply_cosine_fusion
  6.7 0.0 slice-done
  6.7 0.0 slice-done.1
  6.7 0.0 copy-done.3
  6.7 0.9 pad_maximum_fusion.gu_hbm
  7.7 0.0 copy-done.4
  7.7 0.1 copy.26
  7.9 0.1 add_convert_fusion
  8.0 0.0 copy-start
  8.0 0.0 copy-start.1
  8.0 0.2 copy.28
  8.2 0.7 copy.29
  8.9 0.2 convolution_convert_fusion
  9.2 0.1 copy-done
  9.3 0.3 copy-done.1
  9.6 3.1 %bitcast_select_fusion = (bf16[4096,128]{1,0:T(8,128)(2,1)}, bf16[4096,128]{1,0:T(8,128)(2,1)}) fusion(bf16[1,1,32,128,128]{4,3,2,1,0:T(8,128)(2,1)S(1)} %copy-done, pred[4096]{0:T(1024)(128)(4,1)S(1)} %get-tuple-element.21, pred[4096]{0:T(1024)(128)(4,1)S(1)} %get-tuple-element.22, pred[4096]{0:T(1024)(128)(4,1)S(1)} %get-tuple-element.18, ...), kind=kLoop, calls=%fused_computation.1 | loop fusion | flops 3145728 | bytes 4403200 | tf_op jit(solution)/shard_map/jit(_where)/select_n | solution.py:427
  12.8 112.8 %layer.1 = bf16[16,5120]{1,0:T(8,128)(2,1)} custom-call(bf16[2,4,128,128]{3,2,1,0:T(8,128)(2,1)} %bitcast.67, s32[1,4096]{1,0:T(1,128)} %bitcast.73, bf16[16,5120]{1,0:T(8,128)(2,1)} %bitcast.72, bf16[1,5120]{1,0:T(2,128)(2,1)} %broadcast_in_dim.126.gain_ref, bf16[4096,128]{1,0:T(8,128)(2,1)} %get-tuple-element.12.k_hbm, ...), custom_call_target="tpu_custom_call" | custom-call | tf_op jit(solution)/shard_map/layer/pallas_call | solution.py:348
  125.6 0.0 copy-start.2
  125.6 2.8 %select_select_fusion = (bf16[1,1,32,128,128]{4,3,2,1,0:T(8,128)(2,1)}, bf16[1,1,32,128,128]{4,3,2,1,0:T(8,128)(2,1)}) fusion(bf16[1,1,32,128,128]{4,3,2,1,0:T(8,128)(2,1)S(1)} %copy-done, pred[32]{0:T(512)(128)(4,1)S(1)} %get-tuple-element.20, pred[32]{0:T(512)(128)(4,1)S(1)} %get-tuple-element.19, pred[32,128]{1,0:T(8,128)(4,1)S(1)} %get-tuple-element.17, ...), kind=kLoop, calls=%fused_computation.7 | loop fusion | flops 3145728 | bytes 4395072 | tf_op jit(solution)/shard_map/jit(_where)/select_n | solution.py:427
  128.5 0.0 copy-done.2
  128.5 0.7 copy.33
  (10 shorter events, 0.1 us)
Async XLA Ops:
  0.6 6.1 %slice-start = ((bf16[320,448]{1,0:T(8,128)(2,1)}), bf16[320,64]{1,0:T(8,128)(2,1)S(1)}, s32[]{:S(2)}) async-start(bf16[320,448]{1,0:T(8,128)(2,1)} %param.24), calls=%async_computation | async-start | bytes 163840 | tf_op jit(solution)/shard_map/slice | solution.py:432
  0.6 6.1 %slice-start.1 = ((bf16[320,448]{1,0:T(8,128)(2,1)}), bf16[320,384]{1,0:T(8,128)(2,1)S(1)}, s32[]{:S(2)}) async-start(bf16[320,448]{1,0:T(8,128)(2,1)} %param.24), calls=%async_computation.1 | async-start | bytes 491520 | tf_op jit(solution)/shard_map/slice | solution.py:432
  0.7 6.1 %copy-start.3 = (bf16[320,448]{1,0:T(8,128)(2,1)S(1)}, bf16[320,448]{1,0:T(8,128)(2,1)}, u32[]{:S(2)}) copy-start(bf16[320,448]{1,0:T(8,128)(2,1)} %param.23) | copy-start | bytes 860164
  4.5 3.2 %copy-start.4 = (bf16[1,256,512]{2,1,0:T(8,128)(2,1)S(1)}, bf16[1,256,512]{2,1,0:T(8,128)(2,1)}, u32[]{:S(2)}) copy-start(bf16[1,256,512]{2,1,0:T(8,128)(2,1)} %param.14) | copy-start | bytes 786436
  8.0 1.3 %copy-start = (bf16[1,1,32,128,128]{4,3,2,1,0:T(8,128)(2,1)S(1)}, bf16[1,1,32,128,128]{4,3,2,1,0:T(8,128)(2,1)}, u32[]{:S(2)}) copy-start(bf16[1,1,32,128,128]{4,3,2,1,0:T(8,128)(2,1)} %param.18) | copy-start | bytes 3145732
  8.0 1.6 %copy-start.1 = (bf16[1,1,32,128,128]{4,3,2,1,0:T(8,128)(2,1)S(1)}, bf16[1,1,32,128,128]{4,3,2,1,0:T(8,128)(2,1)}, u32[]{:S(2)}) copy-start(bf16[1,1,32,128,128]{4,3,2,1,0:T(8,128)(2,1)} %param.17) | copy-start | bytes 3145732
  125.6 2.9 %copy-start.2 = (bf16[16,5120]{1,0:T(8,128)(2,1)S(1)}, bf16[16,5120]{1,0:T(8,128)(2,1)}, u32[]{:S(2)}) copy-start(bf16[16,5120]{1,0:T(8,128)(2,1)} %layer.1) | copy-start | bytes 491524

commit v2 on v1

v2 whole, which is shorter than its diff:
```python
import functools
import math

import jax
import jax.numpy as jnp
from jax import lax
from jax.experimental import pallas as pl
from jax.experimental.pallas import tpu as pltpu
from jax.sharding import PartitionSpec as P

MESH = pl.DeviceIdType.MESH
SIDE = 4
RING = 8
ROWS = 16
BF16, F32 = jnp.bfloat16, jnp.float32


def torus_plan():
    entries, got = [], {}

    def add(rnd, offset, first, count, direction):
        need = sorted({got[offset, q] for q in range(first, first + count)}) if offset != (0, 0) else []
        there = tuple((o - d) % SIDE for o, d in zip(offset, direction))
        for q in range(first, first + count):
            assert (there, q) not in got and there != (0, 0)
            got[there, q] = len(entries)
        entries.append((rnd, offset, first, count, direction, need))

    east, west, north, south = (1, 0), (-1, 0), (0, 1), (0, -1)
    for direction in (east, west, north, south):
        add(0, (0, 0), 0, 4, direction)
    late = []
    for offset, half, quarters, ahead, across in (
        ((1, 0), 0, (0, 2), west, (north, south)),
        ((3, 0), 0, (1, 3), east, (north, south)),
        ((0, 1), 2, (0, 2), south, (east, west)),
        ((0, 3), 2, (1, 3), north, (east, west)),
    ):
        for quarter in quarters:
            add(1, offset, quarter, 1, ahead)
        for direction in across:
            late.append((1, offset, half, 2, direction))
    for entry in late:
        add(*entry)
    for direction in (north, south):
        add(2, (2, 0), 0, 2, direction)
    for direction in (east, west):
        add(2, (0, 2), 2, 2, direction)
    for offset in ((1, 1), (3, 1), (1, 3), (3, 3)):
        add(2, offset, *((0, 1, south) if offset[1] == 1 else (1, 1, north)))
        add(2, offset, *((2, 1, west) if offset[0] == 1 else (3, 1, east)))
    add(3, (2, 1), 0, 1, south)
    add(3, (2, 3), 1, 1, north)
    add(3, (1, 2), 2, 1, west)
    add(3, (3, 2), 3, 1, east)
    assert len(got) == 4 * (SIDE * SIDE - 1)
    return entries


PLAN = torus_plan()
STREAMS = ((1, 0, 4), (-1, 1, 4), (-1, 0, 3), (1, 1, 3))
BASE = (0, 4, 8, 11)
SLOTS_Z = 14
PLACES = (
    (0, 0), (1, 0), (3, 0), (0, 1), (0, 3), (2, 0), (0, 2), (1, 1), (3, 1), (1, 3),
    (3, 3), (2, 1), (2, 3), (1, 2), (3, 2), (2, 2),
)
EARLY = 10


def kernel(
    q_ref, fresh_k, fresh_v, cos_ref, sin_ref, len_ref, table_ref, x_ref, gain_ref,
    k_hbm, v_hbm, wo_hbm, gate_hbm, up_hbm, dn_hbm,
    out_ref, resid, k_out, v_out,
    q_vm, image, logic, rel_ref, k_vm, v_vm, wo_vm, gate_vm, up_vm, gu_vm, dn_vm, raw, gain_row, dt_vm, mine, theirs, sent, attn, pb, nb, acc, hid,
    snd, rcv, snd2, rcv2, snd3, rcv3, xs, xr,
    local_sem, gu_s, gu_r, dt_s, dt_r, one_s, one_r, z1_s, z1_r, zg_s, zg_r, z2_s, z2_r, z3_s, z3_r,
    chip_s, chip_r, ex_s, ex_r,
):
    req, kz, core = lax.axis_index("req"), lax.axis_index("kv"), lax.axis_index("blk")
    other = 1 - core
    mx, my = lax.rem(req, SIDE), lax.div(req, SIDE)
    width = pb.shape[2]
    half = width // 2
    quarter = width // 4
    heads, half_tokens, head_dim = q_vm.shape[1:]
    tokens = 2 * half_tokens
    partner = (req, kz, other)

    def plane(offset):
        x = lax.rem(mx + (offset[0] % SIDE), SIDE)
        y = lax.rem(my + (offset[1] % SIDE), SIDE)
        return y * SIDE + x

    def ring(step):
        return lax.rem(kz + (step % RING), RING)

    pending = []

    def send(src, dst, ssem, rsem, device):
        copy = pltpu.make_async_remote_copy(
            src_ref=src, dst_ref=dst, send_sem=ssem, recv_sem=rsem, device_id=device, device_id_type=MESH
        )
        copy.start()
        pending.append(copy)

    def arrive(dst, ssem, rsem, device):
        pltpu.make_async_remote_copy(
            src_ref=dst, dst_ref=dst, send_sem=ssem, recv_sem=rsem, device_id=device, device_id_type=MESH
        ).wait_recv()

    shard, units = gate_hbm.shape
    whole = units // 128 * 128
    part = shard // 4
    own_rows = pl.ds(pl.multiple_of(req * shard, 16), shard)
    wo_rows = wo_hbm.shape[0]
    local = [
        pltpu.make_async_copy(k_hbm, k_vm, local_sem.at[0]),
        pltpu.make_async_copy(v_hbm, v_vm, local_sem.at[1]),
        pltpu.make_async_copy(gate_hbm, gate_vm, local_sem.at[2]),
        pltpu.make_async_copy(dn_hbm, dn_vm, local_sem.at[3]),
        pltpu.make_async_copy(
            wo_hbm, wo_vm.at[pl.ds(pl.multiple_of(core * wo_rows, 16), wo_rows)], local_sem.at[4]
        ),
        pltpu.make_async_copy(up_hbm, up_vm, local_sem.at[7]),
    ]
    for n in (2, 5, 0, 1, 3, 4):
        local[n].start()
    barrier = pltpu.get_barrier_semaphore()
    friends = [(plane(d), kz, core) for d in ((1, 0), (-1, 0), (0, 1), (0, -1))]
    friends += [(req, ring(1), core), (req, ring(-1), core), partner]
    for friend in friends:
        pl.semaphore_signal(barrier, inc=1, device_id=friend, device_id_type=MESH)
    pl.semaphore_wait(barrier, len(friends))

    stream = {"gu": (gu_vm, gu_s, gu_r), "dt": (raw, dt_s, dt_r)}
    packed = raw.shape[0] // (SIDE * SIDE)
    tiles = packed // 16
    cuts = [16 * ((tiles * q + 3) // 4) for q in range(5)]
    landed = {"gu": set(), "dt": set()}

    def rows_of(name, offset, first, count):
        offset = tuple(o % SIDE for o in offset)
        if name == "dt":
            return pl.ds(PLACES.index(offset) * packed + cuts[first], cuts[first + count] - cuts[first])
        return pl.ds(pl.multiple_of(plane(offset) * shard + first * part, 16), count * part)

    def land(name, index):
        if index in landed[name]:
            return
        landed[name].add(index)
        full, ssem, rsem = stream[name]
        _, offset, first, count, direction, _ = PLAN[index]
        here = tuple(o - d for o, d in zip(offset, direction))
        back = tuple(-d for d in direction)
        arrive(full.at[rows_of(name, here, first, count)], ssem.at[index], rsem.at[index], (plane(back), kz, core))

    def issue(name, rnd):
        full, ssem, rsem = stream[name]
        for index, (when, offset, first, count, direction, need) in enumerate(PLAN):
            if when != rnd:
                continue
            for earlier in need:
                land(name, earlier)
            there = offset if name == "gu" else tuple(o - d for o, d in zip(offset, direction))
            src = full.at[rows_of(name, offset, first, count)]
            dst = full.at[rows_of(name, there, first, count)]
            send(src, dst, ssem.at[index], rsem.at[index], (plane(direction), kz, core))

    local[2].wait()
    local[5].wait()
    gu_vm[own_rows, :whole] = gate_vm[:, :whole]
    gu_vm[own_rows, whole : whole + 128] = jnp.concatenate([gate_vm[:, whole:], up_vm[:, whole:]], axis=1)
    gu_vm[own_rows, whole + 128 :] = up_vm[:, :whole]
    issue("gu", 0)
    own_wo = wo_vm.at[pl.ds(pl.multiple_of(core * wo_rows, 16), wo_rows)]
    send(wo_hbm, own_wo, one_s.at[0], one_r.at[0], partner)

    cosine = jnp.concatenate([cos_ref[...], cos_ref[...]], axis=1)
    sine = jnp.concatenate([-sin_ref[...], sin_ref[...]], axis=1)

    def turn(rows):
        return rows * cosine + pltpu.roll(rows, head_dim // 2, 1) * sine

    for g in range(heads):
        turned = turn(q_ref[:, g * head_dim : (g + 1) * head_dim].astype(F32)).astype(BF16)
        turned = turned.reshape(RING, 2, ROWS, head_dim)
        for p in range(2):
            q_vm[p, g] = turned[:, p].reshape(half_tokens, head_dim)

    page = 128
    pages = logic.shape[0]
    table_len = table_ref.shape[1]
    length = len_ref[...].astype(F32)
    first_page = jnp.floor(length * (1.0 / page))
    shift = length - first_page * page
    place = lax.broadcasted_iota(jnp.int32, (3 * page, tokens), 0) - lax.broadcasted_iota(
        jnp.int32, (3 * page, tokens), 1
    )
    chosen = jnp.where(place.astype(F32) == shift, 1.0, 0.0).astype(BF16)
    image[:, :head_dim] = jnp.dot(chosen, turn(fresh_k[...].astype(F32)).astype(BF16), preferred_element_type=F32)
    image[:, head_dim:] = jnp.dot(chosen, fresh_v[...], preferred_element_type=F32)
    physical = lax.broadcasted_iota(jnp.int32, (pages, table_len), 0) + core * pages
    ids = lax.broadcasted_iota(jnp.int32, (pages, table_len), 1).astype(F32)
    held = jnp.sum(jnp.where(table_ref[...] == physical, ids, 0.0), axis=1, keepdims=True)
    logic[...] = jnp.broadcast_to(held, logic.shape)
    lanes = lax.broadcasted_iota(jnp.int32, (1, page), 1).astype(F32)
    for s in range(pages):
        rel_ref[:, s * page : (s + 1) * page] = logic[s : s + 1, :] * page - length + lanes
    local[0].wait()
    local[1].wait()
    down_rows = lax.broadcasted_iota(jnp.int32, (page, page), 0).astype(F32)

    def write(s, carry):
        number = logic[pl.ds(s, 1), :]
        index = down_rows + (number * page - length)
        new = (index >= 0.0) & (index < float(tokens))
        which = jnp.broadcast_to(number - first_page, (page, page))
        at = pl.ds(pl.multiple_of(s * page, page), page)
        for cache, low in ((k_vm, 0), (v_vm, head_dim)):
            a, b, c = (image[n * page : (n + 1) * page, low : low + head_dim] for n in range(3))
            picked = jnp.where(which == 0.0, a, jnp.where(which == 1.0, b, c))
            cache[at, :] = jnp.where(new, picked, cache[at, :].astype(F32)).astype(BF16)
        return carry

    lax.fori_loop(0, pages, write, 0)
    saved = [
        pltpu.make_async_copy(k_vm, k_out, local_sem.at[5]),
        pltpu.make_async_copy(v_vm, v_out, local_sem.at[6]),
    ]
    for copy in saved:
        copy.start()

    scale = 1.0 / math.sqrt(head_dim)

    def attend(part_id, result):
        row = lax.broadcasted_iota(jnp.int32, (half_tokens, 1), 0)
        token = ((row // ROWS) * (2 * ROWS) + row % ROWS + part_id * ROWS).astype(F32)
        lane = lax.broadcasted_iota(jnp.int32, (half_tokens, head_dim), 1)

        def head(g, carry):
            score = lax.dot_general(
                q_vm[part_id, g], k_vm[...], (((1,), (1,)), ((), ())), preferred_element_type=F32
            )
            allowed = rel_ref[...] <= token
            score = jnp.where(allowed, score * scale, -1e30)
            top = jnp.max(score, axis=-1, keepdims=True)
            weight = jnp.where(allowed, jnp.exp(score - top), 0.0)
            total = jnp.sum(weight, axis=-1, keepdims=True)
            result[g, :, :head_dim] = jnp.dot(weight.astype(BF16), v_vm[...], preferred_element_type=F32)
            result[g, :, head_dim:] = jnp.where(lane < head_dim // 2, top, total)
            return carry

        lax.fori_loop(0, heads, head, 0)

    attend(other, sent)
    send(sent, theirs, one_s.at[1], one_r.at[1], partner)

    fold = shard // 2
    local[3].wait()
    for n in range(whole // 128):
        raw[n * shard : (n + 1) * shard] = dn_vm[:, n * 128 : (n + 1) * 128]
    raw[packed - fold : packed] = jnp.concatenate([dn_vm[:fold, whole:], dn_vm[fold:, whole:]], axis=1)
    issue("dt", 0)
    attend(core, mine)
    arrive(theirs, one_s.at[1], one_r.at[1], partner)
    mid = head_dim + head_dim // 2
    for g in range(heads):
        a, b = mine[g], theirs[g]
        top_a, top_b = a[:, head_dim : head_dim + 1], b[:, head_dim : head_dim + 1]
        top = jnp.maximum(top_a, top_b)
        fa, fb = jnp.exp(top_a - top), jnp.exp(top_b - top)
        total = fa * a[:, mid : mid + 1] + fb * b[:, mid : mid + 1]
        value = (fa * a[:, :head_dim] + fb * b[:, :head_dim]) / total
        attn[:, g * head_dim : (g + 1) * head_dim] = value.astype(BF16)

    def columns(part_id):
        return slice(part_id * half, (part_id + 1) * half)

    def ring_send(s, j, spans, out_buf, in_buf, ssem, rsem):
        direction, part_id, reach = STREAMS[s]
        start, size = spans[part_id]
        slot = BASE[s] + j
        value = pb[ring(direction * (reach - j)), :, start : start + size]
        if j > 0:
            ring_arrive(s, j - 1, size, in_buf, ssem, rsem)
            value = value + in_buf[slot - 1, :, :size].astype(F32)
        out_buf[slot, :, :size] = value.astype(BF16)
        here, there = out_buf.at[slot, :, :size], in_buf.at[slot, :, :size]
        send(here, there, ssem.at[slot], rsem.at[slot], (req, ring(direction), core))

    def ring_arrive(s, j, size, in_buf, ssem, rsem):
        slot = BASE[s] + j
        there = in_buf.at[slot, :, :size]
        arrive(there, ssem.at[slot], rsem.at[slot], (req, ring(-STREAMS[s][0]), core))

    def ring_total(part_id, spans, out_buf, in_buf, ssem, rsem):
        start, size = spans[part_id]
        value = pb[kz, :, start : start + size]
        for s, (direction, p, reach) in enumerate(STREAMS):
            if p == part_id:
                ring_arrive(s, reach - 1, size, in_buf, ssem, rsem)
                value = value + in_buf[BASE[s] + reach - 1, :, :size].astype(F32)
        return value

    def ring_round(j, part_ids, *buffers):
        for s, (_, p, reach) in enumerate(STREAMS):
            if j < reach and p in part_ids:
                ring_send(s, j, *buffers)

    first = (((0, half), (half, half)), snd, rcv, z1_s, z1_r)
    local[4].wait()
    theirs_wo = wo_vm.at[pl.ds(pl.multiple_of(other * wo_rows, 16), wo_rows)]
    arrive(theirs_wo, one_s.at[0], one_r.at[0], partner)
    for c in range(4):
        cols = slice(c * quarter, (c + 1) * quarter)
        block = jnp.dot(attn[...], wo_vm[:, cols], preferred_element_type=F32)
        pb[:, :, cols] = block.reshape(RING, ROWS, quarter)
        if c % 2 == 1:
            ring_round(0, (c // 2,), *first)
    issue("gu", 1)
    for j in range(1, 4):
        ring_round(j, (0, 1), *first)
    for p in range(2):
        resid[:, columns(p)] = ring_total(p, *first) + x_ref[:, columns(p)].astype(F32)
    gains = gain_ref[...].astype(F32)
    for n in range(gains.shape[0]):
        gain_row[:, n * 128 : (n + 1) * 128] = gains[n : n + 1]
    rows = resid[...]
    inverse = lax.rsqrt(jnp.mean(rows * rows, axis=-1, keepdims=True) + 1e-05)
    nb[kz] = (rows * inverse * gain_row[...]).astype(BF16)

    def chip_send(step, part_id):
        slot = part_id * RING + step % RING
        block = ring(step)
        send(
            nb.at[block, :, columns(part_id)], nb.at[RING + block, :, columns(part_id)],
            chip_s.at[slot], chip_r.at[slot], partner,
        )

    def gather_arrive(s, j):
        direction, part_id, _ = STREAMS[s]
        slot = BASE[s] + j
        step = -direction * (j + 1)
        arrive(nb.at[ring(step), :, columns(part_id)], zg_s.at[slot], zg_r.at[slot], (req, ring(-direction), core))

    def gather_send(s, j):
        direction, part_id, _ = STREAMS[s]
        slot = BASE[s] + j
        block = nb.at[ring(-direction * j), :, columns(part_id)]
        send(block, block, zg_s.at[slot], zg_r.at[slot], (req, ring(direction), core))

    order = (0, 2, 1, 3)
    for s in order:
        gather_send(s, 0)
    for p in range(2):
        chip_send(0, p)
    for j in range(1, 4):
        for s in order:
            direction, part_id, reach = STREAMS[s]
            gather_arrive(s, j - 1)
            if j < reach:
                gather_send(s, j)
            chip_send(-direction * j, part_id)
        if j == 2:
            issue("gu", 2)
    for s in (0, 1):
        direction, part_id, reach = STREAMS[s]
        gather_arrive(s, reach - 1)
        chip_send(-direction * reach, part_id)
    issue("gu", 3)
    issue("dt", 1)
    for index in range(len(PLAN)):
        land("gu", index)

    for c in range(4):
        if c % 2 == 0:
            for step in range(RING):
                slot = (c // 2) * RING + step
                block = nb.at[RING + ring(step), :, columns(c // 2)]
                arrive(block, chip_s.at[slot], chip_r.at[slot], partner)
        cols = slice(c * quarter, (c + 1) * quarter)
        value = jnp.dot(
            nb[:, :, cols].reshape(2 * RING * ROWS, quarter), gu_vm[cols, :], preferred_element_type=F32
        )
        if c == 0:
            acc[...] = value
        else:
            acc[...] += value
    gate, up = acc[:, :whole], acc[:, whole + 128 :]
    hid[:, :whole] = (gate / (1.0 + jnp.exp(-gate)) * up).astype(BF16)
    gate = acc[:, whole : whole + 128]
    up = pltpu.roll(gate, 64, 1)
    tail = (gate / (1.0 + jnp.exp(-gate)) * up).astype(BF16)
    hid[:, whole:] = tail[:, : units - whole]

    lead = EARLY * shard

    def unpack(place):
        start = place * packed
        rows = slice(place * shard, (place + 1) * shard)
        for n in range(whole // 128):
            dt_vm[rows, n * 128 : (n + 1) * 128] = raw[start + n * shard : start + (n + 1) * shard]
        tail = raw[start + packed - fold : start + packed]
        dt_vm[rows.start : rows.start + fold, whole:] = tail[:, : units - whole]
        tail = pltpu.roll(tail.astype(F32), 64, 1).astype(BF16)
        dt_vm[rows.start + fold : rows.stop, whole:] = tail[:, : units - whole]

    def multiply(spans, slot):
        for p, (start, size) in enumerate(spans):
            cols = slice(start, start + size)
            value = lax.dot_general(
                hid[...], dt_vm[cols, :], (((1,), (1,)), ((), ())), preferred_element_type=F32
            )
            pb[:, :, cols] = value[: RING * ROWS].reshape(RING, ROWS, size)
            xs[:, :, cols] = value[RING * ROWS :].astype(BF16).reshape(RING, ROWS, size)
            send(xs.at[:, :, cols], xr.at[:, :, cols], ex_s.at[slot + p], ex_r.at[slot + p], partner)

    def combine(part_id, spans, slot):
        start, size = spans[part_id]
        cols = slice(start, start + size)
        arrive(xr.at[:, :, cols], ex_s.at[slot + part_id], ex_r.at[slot + part_id], partner)
        pb[:, :, cols] += xr[:, :, cols].astype(F32)

    second = (((0, 1664), (1664, lead - 1664)), snd2, rcv2, z2_s, z2_r)
    third = (((lead, 1024), (lead + 1024, width - lead - 1024)), snd3, rcv3, z3_s, z3_r)
    issue("dt", 2)
    for index, entry in enumerate(PLAN):
        if entry[0] < 2:
            land("dt", index)
    for place in range(EARLY):
        unpack(place)
    multiply(second[0], 0)
    for p in range(2):
        combine(p, second[0], 0)
        ring_round(0, (p,), *second)
    issue("dt", 3)
    ring_round(1, (0, 1), *second)
    for index in range(len(PLAN)):
        land("dt", index)
    for place in range(EARLY, SIDE * SIDE):
        unpack(place)
    multiply(third[0], 2)
    ring_round(2, (0, 1), *second)
    for p in range(2):
        combine(p, third[0], 2)
        ring_round(0, (p,), *third)
    ring_round(3, (0, 1), *second)
    ring_round(1, (0, 1), *third)

    def finish(places, *buffers):
        for p, (start, size) in enumerate(buffers[0]):
            pb[0, :, start : start + size] = ring_total(p, *buffers)
        for place in places:
            start = place * shard
            skew = start % 128
            span = -(-(skew + shard) // 128) * 128
            block = pb[0, :, start - skew : start - skew + span]
            if skew:
                block = pltpu.roll(block, span - skew, 1)
            out_ref[plane(PLACES[place])] = block[:, :shard]

    ring_round(2, (0, 1), *third)
    ring_round(3, (0, 1), *third)
    finish(range(EARLY), *second)
    finish(range(EARLY, SIDE * SIDE), *third)
    for copy in saved:
        copy.wait()
    for copy in pending:
        copy.wait_send()


def layer(q, fresh_k, fresh_v, cosine, sine, length, table, x, gain, keys, values, wo, gate, up, down):
    width = x.shape[1]
    out_part, hidden = down.shape
    slots, head_dim = keys.shape
    pages = slots // 128
    tokens, heads = q.shape[0], q.shape[1] // head_dim
    vmem = pl.BlockSpec(memory_space=pltpu.VMEM)
    hbm = pl.BlockSpec(memory_space=pl.ANY)
    dma = pltpu.SemaphoreType.DMA
    part = pltpu.VMEM((heads, tokens // 2, 2 * head_dim), F32)
    hops = [pltpu.VMEM((SLOTS_Z, ROWS, size), BF16) for size in (width // 2, 1664, 1024)]
    plan = dma((len(PLAN),))
    packed = hidden * out_part // 128
    cache = jax.ShapeDtypeStruct(keys.shape, BF16)
    return pl.pallas_call(
        kernel,
        out_shape=(
            jax.ShapeDtypeStruct((SIDE * SIDE, ROWS, out_part), F32),
            jax.ShapeDtypeStruct(x.shape, F32),
            cache,
            cache,
        ),
        in_specs=[vmem] * 9 + [hbm] * 6,
        out_specs=(vmem, vmem, hbm, hbm),
        scratch_shapes=[
            pltpu.VMEM((2, heads, tokens // 2, head_dim), BF16),
            pltpu.VMEM((3 * 128, 2 * head_dim), F32),
            pltpu.VMEM((pages, 128), F32),
            pltpu.VMEM((1, slots), F32),
            pltpu.VMEM((slots, head_dim), BF16),
            pltpu.VMEM((slots, head_dim), BF16),
            pltpu.VMEM((2 * wo.shape[0], width), BF16),
            pltpu.VMEM(gate.shape, BF16),
            pltpu.VMEM(up.shape, BF16),
            pltpu.VMEM((width, 2 * hidden), BF16),
            pltpu.VMEM(down.shape, BF16),
            pltpu.VMEM((SIDE * SIDE * packed, 128), BF16),
            pltpu.VMEM((1, width), F32),
            pltpu.VMEM((width, hidden), BF16),
            part, part, part,
            pltpu.VMEM((tokens // 2, heads * head_dim), BF16),
            pltpu.VMEM((RING, ROWS, width), F32),
            pltpu.VMEM((2 * RING, ROWS, width), BF16),
            pltpu.VMEM((2 * RING * ROWS, 2 * hidden), F32),
            pltpu.VMEM((2 * RING * ROWS, hidden), BF16),
            hops[0], hops[0], hops[1], hops[1], hops[2], hops[2],
            pltpu.VMEM((RING, ROWS, width), BF16),
            pltpu.VMEM((RING, ROWS, width), BF16),
            dma((8,)),
            plan, plan, plan, plan,
            dma((2,)), dma((2,)),
            *[dma((SLOTS_Z,))] * 8,
            dma((2 * RING,)), dma((2 * RING,)),
            dma((4,)), dma((4,)),
        ],
        compiler_params=pltpu.CompilerParams(
            collective_id=0, has_side_effects=True, vmem_limit_bytes=62 * 2**20
        ),
        name="layer",
    )(q, fresh_k, fresh_v, cosine, sine, length, table, x, gain, keys, values, wo, gate, up, down)


def on_device(
    x_resid, q_new, k_new, v_new, k_cache, v_cache, cache_len, page_table, wo, norm_gain, w_gate, w_up, w_down
):
    new_tokens, head_dim = k_new.shape[1:]
    half = head_dim // 2
    positions = cache_len[0] + jnp.arange(new_tokens, dtype=jnp.int32)
    frequency = jnp.power(1000000.0, -2.0 * jnp.arange(half, dtype=F32) / head_dim)
    angles = positions.astype(F32)[:, None] * frequency[None, :]
    mlp, resid, keys, values = layer(
        q_new[0],
        k_new[0],
        v_new[0],
        jnp.cos(angles),
        jnp.sin(angles),
        cache_len[None],
        page_table,
        x_resid[0],
        norm_gain.reshape(-1, 128),
        k_cache.reshape(-1, head_dim),
        v_cache.reshape(-1, head_dim),
        wo,
        w_gate,
        w_up,
        w_down.T,
    )
    mlp = mlp.transpose(1, 0, 2).reshape(resid.shape)
    layer_out = (resid + mlp).astype(BF16)[None]
    return (layer_out, keys.reshape(k_cache.shape), values.reshape(v_cache.shape))


def solution(mesh):
    in_specs = (
        P("req", ("kv", "blk"), None),
        P("req", None, "kv"),
        P("req", None, "kv"),
        P("req", None, "kv"),
        P("req", "kv", "blk", None, None),
        P("req", "kv", "blk", None, None),
        P("req"),
        P("req", None),
        P(("kv", "blk"), None),
        P(),
        P("req", ("kv", "blk")),
        P("req", ("kv", "blk")),
        P(("kv", "blk"), "req"),
    )
    out_specs = (
        P("req", ("kv", "blk"), None),
        P("req", "kv", "blk", None, None),
        P("req", "kv", "blk", None, None),
    )
    return jax.shard_map(on_device, mesh=mesh, in_specs=in_specs, out_specs=out_specs, check_vma=False)
```

time: 129 us -> 116 us (0.90)
  other arithmetic: 9.02 us -> 2.92 us
  Pallas kernels: 113 us -> 108 us
  local copies, waits for them, and re-layouts: 5.46 us -> 3.36 us
    select_n x2 -> x0, other arithmetic: 5.99 us -> none  [written(): return jnp.where(is_new, picked, cache[0, 0])]
    pallas_call x1, Pallas kernels: 113 us -> 108 us  [layer(): pl.pallas_call(kernel, out_shape=(jax.ShapeDtypeStruct((SIDE * SIDE, ROWS...]
    broadcast_in_dim x0 -> x1, other arithmetic: none -> 1.67 us  [on_device(): layer_out = (resid + mlp).astype(BF16)[None]]
    broadcast_in_dim x2 -> x0, local copies, waits for them, and re-layouts: 1.39 us -> none  [the longest x1 1.32 us: on_device(): norm_gain[None]]
    unnamed x14 -> x6, local copies, waits for them, and re-layouts: 3.13 us -> 1.95 us
where the time goes in v2:
time: 116 us
  Pallas kernels  108 us (93%)
  local copies, waits for them, and re-layouts  3.36 us (3%)
  other arithmetic  2.92 us (3%)
  between operations  1.32 us (1%)
    pallas_call x1, Pallas kernels, layer(): pl.pallas_call(kernel, out_shape=(jax.ShapeDtypeStruct((SIDE * SIDE, ROWS...  108 us

profile of v2, /device:TPU:32, one launch (start us, length us, event | category | flops | bytes accessed | tf_op | source)
XLA Modules:
  0.0 115.6 jit_solution(5777850898332490694)
XLA Ops:
  1.3 1.2 %multiply_sine_fusion = (f32[256,64]{1,0:T(8,128)}, f32[256,64]{1,0:T(8,128)}) fusion(f32[64]{0:T(128)S(1)} %multiply_power_fusion, f32[256]{0:T(256)S(1)} %add_convert_fusion.1), kind=kLoop, calls=%fused_computation.1 | loop fusion | flops 16384 | bytes 132352 | tf_op jit(solution)/shard_map/sin | solution.py:548
  2.5 108.0 %layer.1 = (f32[16,16,320]{2,1,0:T(8,128)}, f32[16,5120]{1,0:T(8,128)}, bf16[4096,128]{1,0:T(8,128)(2,1)}, bf16[4096,128]{1,0:T(8,128)(2,1)}) custom-call(bf16[256,512]{1,0:T(8,128)(2,1)} %bitcast.23, bf16[256,128]{1,0:T(8,128)(2,1)} %bitcast.25, bf16[256,128]{1,0:T(8,128)(2,1)} %bitcast.26, f32[256,64]{1,0:T(8,128)} %get-tuple-element.12.cos_ref, ...), custom_call_target="tpu_custom_call" | custom-call | tf_op jit(solution)/shard_map/layer/pallas_call | solution.py:487
  110.6 0.0 copy-start.1
  110.6 0.0 copy-start
  110.6 1.3 %copy.16 = f32[16,16,320]{2,1,0:T(8,128)S(1)} copy(f32[16,16,320]{2,0,1:T(8,128)} %bitcast.21) | data formatting | bytes 655360 | tf_op jit(solution)/shard_map/transpose | solution.py:560
  111.9 0.1 reshape.37
  112.0 1.7 %fusion = bf16[1,16,5120]{2,1,0:T(8,128)(2,1)} fusion(f32[16,5120]{1,0:T(8,128)} %get-tuple-element.7, f32[16,5120]{1,0:T(8,128)S(1)} %reshape.37), kind=kLoop, calls=%fused_computation.3 | loop fusion | flops 163840 | bytes 819200 | tf_op jit(solution)/shard_map/broadcast_in_dim | solution.py:561
  113.7 0.0 copy-done.1
  113.7 1.0 copy.20
  114.7 0.0 copy-done
  114.7 1.0 copy.21
  (2 shorter events, 0.0 us)
Async XLA Ops:
  110.6 3.1 %copy-start.1 = (bf16[4096,128]{1,0:T(8,128)(2,1)S(1)}, bf16[4096,128]{1,0:T(8,128)(2,1)}, u32[]{:S(2)}) copy-start(bf16[4096,128]{1,0:T(8,128)(2,1)} %get-tuple-element.9) | copy-start | bytes 3145732
  110.6 4.1 %copy-start = (bf16[4096,128]{1,0:T(8,128)(2,1)S(1)}, bf16[4096,128]{1,0:T(8,128)(2,1)}, u32[]{:S(2)}) copy-start(bf16[4096,128]{1,0:T(8,128)(2,1)} %get-tuple-element.10) | copy-start | bytes 3145732
